TPU v7x, 32 devices: a whole 2x2x4 slice. The times are simulated.
32 devices in a mesh: groups: 2 (over x), blk: 16 (over z, y, core).
Axes of the slice: x: 2, y: 2, z: 4, core: 2. Of those that a mesh axis runs over, the one named last changes fastest.
Arguments:
- queries: bfloat16 [16384, 1536], P(('groups', 'blk')), parts along dimension 0, may hold values from -8 to 8
- key_rows: bfloat16 [16384, 1536], P(('groups', 'blk')), parts along dimension 0, may hold values from -8 to 8
- value_rows: bfloat16 [16384, 1536], P(('groups', 'blk')), parts along dimension 0, may hold values from -24 to 24
- block_mask: int32 [64, 20], P('blk'), may hold values from 0 to 1, as said below
- out_weight: bfloat16 [1536, 3072], P(None, 'blk'), may hold values from -0.5 to 0.5
Outputs:
- projected: bfloat16 [16384, 3072], P(('groups', 'blk')), parts along dimension 0
There are 2 independent parts, one for each index of `groups`. A program takes and returns all parts, laid end to end along the dimension named above; an argument that names none is the same for every part. Nothing has to cross between parts.
Inputs may be any that keep to these rules, and one draw needn't show every extreme that they name: `block_mask`: entry [b, (d + 2) * 4 + j] is 1 if query block b may attend key block j of the slab d slabs after its own in cyclic order (before it for negative d). A slab's own blocks are always admitted. For d = 2 and d = -2, the query blocks of one slab together admit exactly 2 of that slab's key blocks, in every draw.
All inputs are finite; a program needn't handle non-finite values.
Results may differ from a plain program's by a relative error of at most 0.009.
Values may be sent and summed in bfloat16 or wider, within the bound.
A program may use at most 192 MiB of HBM per device.

v0:
```python
import math

import jax
import jax.numpy as jnp
from jax import lax
from jax.sharding import PartitionSpec as P

HEADS = 12
BLOCK = 128
RADIUS = 2


neg_large = -1e30


def shifted(value, axis, steps):
    count = lax.axis_size(axis)
    pairs = [(source, (source + steps) % count) for source in range(count)]
    return lax.ppermute(value, axis, pairs)


def absorb(carried, queries, key_part, value_part, allowed):
    run_max, run_sum, accumulated = carried
    tok_rows = queries.shape[0]
    head_count = HEADS
    head_size = queries.shape[1] // head_count
    key_count = key_part.shape[0]
    block_len = BLOCK
    query_heads = queries.reshape(tok_rows, head_count, head_size)
    key_heads = key_part.reshape(key_count, head_count, head_size)
    value_heads = value_part.reshape(key_count, head_count, head_size)
    scores = jnp.einsum(
        "qhe,khe->hqk", query_heads, key_heads, preferred_element_type=jnp.float32
    ) * (1.0 / math.sqrt(head_size))
    shaped = scores.reshape(
        head_count, tok_rows // block_len, block_len, key_count // block_len, block_len
    )
    keeping = (allowed > 0)[None, :, None, :, None]
    shaped = jnp.where(keeping, shaped, neg_large)
    new_max = jnp.maximum(run_max, jnp.max(shaped, axis=(3, 4)).reshape(head_count, tok_rows))
    level = new_max.reshape(head_count, tok_rows // block_len, block_len)[:, :, :, None, None]
    weights = jnp.where(keeping, jnp.exp(shaped - level), 0.0)
    factor = jnp.exp(run_max - new_max)
    run_sum = run_sum * factor + jnp.sum(weights, axis=(3, 4)).reshape(head_count, tok_rows)
    rounded_probs = weights.reshape(head_count, tok_rows, key_count).astype(jnp.bfloat16)
    update = jnp.einsum(
        "hqk,khe->qhe", rounded_probs, value_heads, preferred_element_type=jnp.float32
    )
    accumulated = accumulated * jnp.transpose(factor)[:, :, None] + update
    return (new_max, run_sum, accumulated)


def local(queries, key_rows, value_rows, block_mask, out_weight):
    tok_rows, feat_width = queries.shape
    head_count = HEADS
    radius = RADIUS
    per_slab = tok_rows // BLOCK
    key_value = jnp.stack((key_rows, value_rows))

    def columns(offset):
        return block_mask[:, (offset + radius) * per_slab : (offset + radius + 1) * per_slab]

    carried = (
        jnp.full((head_count, tok_rows), neg_large, jnp.float32),
        jnp.zeros((head_count, tok_rows), jnp.float32),
        jnp.zeros((tok_rows, head_count, feat_width // head_count), jnp.float32),
    )
    carried = absorb(carried, queries, key_rows, value_rows, columns(0))
    for direction in (1, -1):
        offset = direction
        arrived = shifted(key_value, "blk", -offset)
        carried = absorb(carried, queries, arrived[0], arrived[1], columns(offset))
    far_count = per_slab // 2
    blocked = key_value.reshape(2, per_slab, BLOCK, feat_width)
    for direction in (1, -1):
        offset = direction * radius
        wanted = columns(offset)
        used_any = jnp.max(wanted, axis=0)
        ranking = jnp.argsort((1 - used_any) * per_slab + jnp.arange(per_slab, dtype=jnp.int32))
        picked = ranking[:far_count]
        requests = shifted(picked, "blk", offset)
        chosen = jnp.take(blocked, requests, axis=1).reshape(2, far_count * BLOCK, feat_width)
        arrived = shifted(chosen, "blk", -offset)
        carried = absorb(carried, queries, arrived[0], arrived[1], jnp.take(wanted, picked, axis=1))
    run_max, run_sum, accumulated = carried
    attention = (
        (accumulated / jnp.transpose(run_sum)[:, :, None])
        .reshape(tok_rows, feat_width)
        .astype(jnp.bfloat16)
    )
    result = jnp.dot(
        attention,
        lax.all_gather(out_weight, "blk", axis=1, tiled=True),
        preferred_element_type=jnp.float32,
    )
    return result.astype(jnp.bfloat16)


def solution(mesh):
    in_specs = (
        P(("groups", "blk"), None),
        P(("groups", "blk"), None),
        P(("groups", "blk"), None),
        P("blk", None),
        P(None, "blk"),
    )
    out_specs = P(("groups", "blk"), None)
    return jax.shard_map(local, mesh=mesh, in_specs=in_specs, out_specs=out_specs, check_vma=False)
```

profile of v0, /device:TPU:12, one launch (start us, length us, event | category | flops | bytes accessed | tf_op | source)
XLA Modules:
  0.0 283.0 jit_solution(4080492890166236329)
XLA Ops:
  6.5 1.7 copy.82
  8.3 1.7 copy.86
  10.0 2.1 pad_maximum_fusion
  12.1 1.7 collective-permute-start
  14.0 0.7 sort.32
  14.7 1.4 collective-permute-start.4
  16.2 0.7 sort.31
  16.9 1.5 collective-permute-start.2
  18.6 0.6 gather_fusion.2
  19.4 1.7 copy.81
  21.3 3.8 %pad_maximum_fusion.1 = bf16[2,4,128,1536]{3,2,1,0:T(8,128)(2,1)} fusion(bf16[1,4,128,1536]{3,2,1,0:T(8,128)(2,1)} %bitcast.263, bf16[1,4,128,1536]{3,2,1,0:T(8,128)(2,1)} %bitcast.264), kind=kLoop, calls=%fused_computation.39 | loop fusion | flops 1572864 | bytes 6291456 | tf_op jit(solution)/shard_map/stack | solution.py:58
  25.1 0.6 gather_fusion
  25.7 114.2 %collective-permute-done.4 = s32[2]{0:T(128)S(1)} collective-permute-done((s32[2]{0:T(128)S(1)}, s32[2]{0:T(128)S(1)}, u32[]{:S(2)}, u32[]{:S(2)}) %collective-permute-start.4) | collective-permute-done | bytes 40 | tf_op jit(solution)/shard_map/ppermute | solution.py:19
  139.9 3.7 %gather_fusion.3 = bf16[2,2,128,1536]{3,2,1,0:T(8,128)(2,1)} fusion(bf16[2,4,128,1536]{3,2,1,0:T(8,128)(2,1)} %pad_maximum_fusion.1, s32[1024]{0:T(1024)S(1)} %pad_clamp_fusion), kind=kCustom, calls=%fused_computation.3.clone | custom fusion | bytes 3145736 | tf_op jit(solution)/shard_map/jit(_take)/gather | solution.py:82
  143.7 1.6 select_bitcast_fusion
  145.3 1.2 copy.106
  146.5 3.3 %collective-permute-start.5 = (bf16[2,256,1536]{2,1,0:T(8,128)(2,1)}, bf16[2,256,1536]{2,1,0:T(8,128)(2,1)}, u32[]{:S(2)}, u32[]{:S(2)}) collective-permute-start(bf16[2,256,1536]{2,1,0:T(8,128)(2,1)} %bitcast.29), channel_id=1, source_target_pairs={{0,2},{1,3},{2,4},{3,5},{4,6},{5,7},{6,8},{7,9},{8,10},{9,11},{10,... | collective-permute-start | bytes 4718600 | tf_op jit(solution)/shard_map/ppermute | solution.py:19
  149.9 3.7 %gather_fusion.1 = bf16[2,2,128,1536]{3,2,1,0:T(8,128)(2,1)} fusion(bf16[2,4,128,1536]{3,2,1,0:T(8,128)(2,1)} %pad_maximum_fusion.1, s32[1024]{0:T(1024)S(1)} %pad_clamp_fusion.2), kind=kCustom, calls=%fused_computation.1.clone | custom fusion | bytes 3145736 | tf_op jit(solution)/shard_map/jit(_take)/gather | solution.py:82
  153.6 1.6 select_bitcast_fusion.1
  155.2 1.2 copy.99
  156.7 0.7 copy.145
  158.2 0.9 copy.142
  159.2 0.2 broadcast_in_dim.122
  159.6 7.5 %fusion = (f32[12,512]{1,0:T(8,128)}, f32[12,512,512]{1,2,0:T(8,128)}) fusion(pred[512,512]{0,1:T(8,128)(4,1)S(1)} %bitcast.274, bf16[512,12,128]{0,2,1:T(8,128)(2,1)S(1)} %bitcast.252, bf16[512,12,128]{0,2,1:T(8,128)(2,1)S(1)} %bitcast.262), kind=kOutput, calls=%fused_computation.10 | convolution fusion | flops 814737408 | bytes 16015360 | tf_op jit(solution)/shard_map/qhe,khe->hqk/dot_general | solution.py:32
  167.1 17.4 %collective-permute-done.5 = bf16[2,256,1536]{2,1,0:T(8,128)(2,1)} collective-permute-done((bf16[2,256,1536]{2,1,0:T(8,128)(2,1)}, bf16[2,256,1536]{2,1,0:T(8,128)(2,1)}, u32[]{:S(2)}, u32[]{:S(2)}) %collective-permute-start.5) | collective-permute-done | bytes 1572896 | tf_op jit(solution)/shard_map/ppermute | solution.py:19
  184.5 2.4 fusion.75
  186.8 0.3 copy.107
  187.1 2.6 fusion.76
  189.8 1.4 copy.100
  191.2 2.3 copy.103
  193.4 2.3 copy.110
  195.7 1.3 fusion.19
  197.1 1.3 fusion.18
  198.4 5.5 %fusion.74 = (bf16[1,512,1536]{1,2,0:T(8,128)(2,1)}, bf16[1,512,1536]{1,2,0:T(8,128)(2,1)S(1)}) fusion(bf16[2,512,1536]{1,2,0:T(8,128)(2,1)} %collective-permute-done.1), kind=kLoop, calls=%fused_computation.129 | loop fusion | bytes 6291456 | tf_op jit(solution)/shard_map/slice | solution.py:72
  203.8 3.2 %fusion.73 = (bf16[1,512,1536]{1,2,0:T(8,128)(2,1)}, bf16[1,512,1536]{1,2,0:T(8,128)(2,1)S(1)}) fusion(bf16[2,512,1536]{1,2,0:T(8,128)(2,1)} %collective-permute-done), kind=kLoop, calls=%fused_computation.128 | loop fusion | bytes 6291456 | tf_op jit(solution)/shard_map/slice | solution.py:72
  207.1 2.3 fusion.2
  209.4 7.0 %fusion.1 = (f32[12,512]{1,0:T(8,128)S(1)}, f32[12,512,512]{2,1,0:T(8,128)}) fusion(pred[512,512]{0,1:T(8,128)(4,1)S(1)} %bitcast.277, bf16[512,12,128]{0,2,1:T(8,128)(2,1)S(1)} %bitcast.268, bf16[512,12,128]{0,2,1:T(8,128)(2,1)S(1)} %bitcast.256), kind=kOutput, calls=%fused_computation.11 | convolution fusion | flops 814737408 | bytes 16015360 | tf_op jit(solution)/shard_map/qhe,khe->hqk/dot_general | solution.py:32
  216.5 1.5 fusion.20
  218.0 1.5 fusion.22
  219.6 7.5 %fusion.5 = f32[12,512]{1,0:T(8,128)S(1)} fusion(f32[12,512,512]{2,1,0:T(8,128)} %get-tuple-element.48, f32[12,512]{1,0:T(8,128)S(1)} %get-tuple-element.20, pred[512,512]{0,1:T(8,128)(4,1)S(1)} %bitcast.278), kind=kLoop, calls=%fused_computation.15 | loop fusion | flops 15722496 | bytes 12894208 | tf_op jit(solution)/shard_map/reduce_sum | solution.py:44
  227.1 3.2 %fusion.7 = f32[12,512]{1,0:T(8,128)S(1)} fusion(f32[12,512,512]{2,1,0:T(8,128)S(1)} %get-tuple-element.46, f32[12,512]{1,0:T(8,128)S(1)} %get-tuple-element.19, pred[512,512]{0,1:T(8,128)(4,1)S(1)} %bitcast.272), kind=kLoop, calls=%fused_computation.17 | loop fusion | flops 15722496 | bytes 12894208 | tf_op jit(solution)/shard_map/reduce_sum | solution.py:44
  230.4 3.2 %fusion.3 = f32[12,512]{1,0:T(8,128)S(1)} fusion(f32[12,512,512]{1,2,0:T(8,128)S(1)} %bitcast.258, f32[12,512]{1,0:T(8,128)S(1)} %get-tuple-element.35, pred[512,512]{0,1:T(8,128)(4,1)S(1)} %bitcast.275), kind=kLoop, calls=%fused_computation.13 | loop fusion | flops 15722496 | bytes 12894208 | tf_op jit(solution)/shard_map/reduce_sum | solution.py:44
  233.7 3.7 %fusion.26 = f32[12,128,512]{2,1,0:T(8,128)} fusion(bf16[256,12,128]{0,2,1:T(8,128)(2,1)S(1)} %bitcast.292, f32[12,256,512]{2,1,0:T(8,128)S(1)} %bitcast.260, f32[12,512]{1,0:T(8,128)S(1)} %get-tuple-element.18, pred[512,256]{0,1:T(8,128)(4,1)S(1)} %bitcast.287), kind=kOutput, calls=%fused_computation.37 | convolution fusion | flops 410517504 | bytes 10379264 | tf_op jit(solution)/shard_map/hqk,khe->qhe/dot_general | solution.py:46
  237.4 9.9 %fusion.11 = f32[12,128,512]{2,1,0:T(8,128)} fusion(bf16[512,12,128]{0,2,1:T(8,128)(2,1)S(1)} %bitcast.281, f32[12,512,512]{2,1,0:T(8,128)} %get-tuple-element.48, f32[12,512]{1,0:T(8,128)S(1)} %get-tuple-element.20, pred[512,512]{0,1:T(8,128)(4,1)S(1)} %bitcast.279), kind=kOutput, calls=%fused_computation.24 | convolution fusion | flops 821035008 | bytes 17588224 | tf_op jit(solution)/shard_map/hqk,khe->qhe/dot_general | solution.py:46
  247.2 6.3 %fusion.9 = f32[12,128,512]{2,1,0:T(8,128)} fusion(bf16[512,12,128]{0,2,1:T(8,128)(2,1)} %bitcast.280, f32[12,512,512]{2,1,0:T(8,128)S(1)} %get-tuple-element.46, f32[12,512]{1,0:T(8,128)S(1)} %get-tuple-element.19, pred[512,512]{0,1:T(8,128)(4,1)S(1)} %bitcast.273), kind=kOutput, calls=%fused_computation.23 | convolution fusion | flops 821035008 | bytes 17588224 | tf_op jit(solution)/shard_map/hqk,khe->qhe/dot_general | solution.py:46
  253.5 4.8 %fusion.13 = f32[12,512,128]{1,2,0:T(8,128)} fusion(bf16[512,12,128]{0,2,1:T(8,128)(2,1)S(1)} %bitcast.266, f32[12,512,512]{1,2,0:T(8,128)S(1)} %bitcast.258, f32[12,512]{1,0:T(8,128)S(1)} %get-tuple-element.35, pred[512,512]{0,1:T(8,128)(4,1)S(1)} %bitcast.276), kind=kOutput, calls=%fused_computation.25 | convolution fusion | flops 821035008 | bytes 17588224 | tf_op jit(solution)/shard_map/hqk,khe->qhe/dot_general | solution.py:46
  258.4 7.5 %fusion.29 = bf16[512,12,128]{0,2,1:T(8,128)(2,1)S(1)} fusion(f32[12,128,512]{2,1,0:T(8,128)S(1)} %copy-done.14, f32[12,128,512]{2,1,0:T(8,128)} %fusion.9, f32[12,128,512]{2,1,0:T(8,128)S(1)} %copy-done.15, f32[12,512,128]{1,2,0:T(8,128)} %fusion.13, f32[512,12]{0,1:T(8,128)S(1)} %get-tuple-element.13, f32[512,12]{0,1:T(8,128)S(1)} %get-tuple-element.16, ...), kind=kOutput, calls=%fused_computation.42 | convolution fusion | flops 419168256 | bytes 21536768 | tf_op jit(solution)/shard_map/hqk,khe->qhe/dot_general | solution.py:46
  266.0 10.2 %convolution_convert_fusion = bf16[512,3072]{1,0:T(8,128)(2,1)} fusion(bf16[512,1536]{0,1:T(8,128)(2,1)S(1)} %bitcast.297, bf16[1536,3072]{0,1:T(8,128)(2,1)} %all-gather.2.cloned.1.call-done), kind=kOutput, calls=%fused_computation.31 | convolution fusion | flops 4833411072 | bytes 14155776 | tf_op jit(solution)/shard_map/dot_general | solution.py:91
  (84 shorter events, 2.1 us)
Async XLA Ops:
  6.5 7.4 %copy-start.13 = (s32[4,20]{1,0:T(4,128)S(1)}, s32[4,20]{1,0:T(4,128)}, u32[]{:S(2)}) copy-start(s32[4,20]{1,0:T(4,128)} %param.12) | copy-start | bytes 964
  6.5 259.4 %all-gather.2.cloned.1.call-start = ((), (), s32[]{:S(2)}) async-start(), calls=%async_computation | async-start | bytes 10027008 | tf_op jit(solution)/shard_map/all_gather | solution.py:93
  10.0 9.4 %copy-start.2 = (bf16[512,1536]{0,1:T(8,128)(2,1)}, bf16[512,1536]{0,1:T(8,128)(2,1)S(1)}, u32[]{:S(2)}) copy-start(bf16[512,1536]{0,1:T(8,128)(2,1)S(1)} %copy.86) | copy-start | bytes 4718596
  12.1 186.2 %collective-permute-start.1 = (bf16[2,512,1536]{1,2,0:T(8,128)(2,1)}, bf16[2,512,1536]{1,2,0:T(8,128)(2,1)}, u32[]{:S(2)}, u32[]{:S(2)}) collective-permute-start(bf16[2,512,1536]{1,2,0:T(8,128)(2,1)} %pad_maximum_fusion), channel_id=1, source_target_pairs={{0,1},{1,2},{2,3},{3,4},{4,5},{5,6},{6,7},{7,8},{8,9},{9,10},{10,1... | collective-permute-start | bytes 9437192 | tf_op jit(solution)/shard_map/ppermute | solution.py:19
  12.1 191.7 %collective-permute-start = (bf16[2,512,1536]{1,2,0:T(8,128)(2,1)}, bf16[2,512,1536]{1,2,0:T(8,128)(2,1)}, u32[]{:S(2)}, u32[]{:S(2)}) collective-permute-start(bf16[2,512,1536]{1,2,0:T(8,128)(2,1)} %pad_maximum_fusion), channel_id=1, source_target_pairs={{0,15},{1,0},{2,1},{3,2},{4,3},{5,4},{6,5},{7,6},{8,7},{9,8},{10,9... | collective-permute-start | bytes 9437192 | tf_op jit(solution)/shard_map/ppermute | solution.py:19
  14.7 125.1 %collective-permute-start.4 = (s32[2]{0:T(128)S(1)}, s32[2]{0:T(128)S(1)}, u32[]{:S(2)}, u32[]{:S(2)}) collective-permute-start(s32[2]{0:T(128)S(1)} %bitcast.296), channel_id=1, source_target_pairs={{0,14},{1,15},{2,0},{3,1},{4,2},{5,3},{6,4},{7,5},{8,6},{9,7},{10,... | collective-permute-start | bytes 32 | tf_op jit(solution)/shard_map/ppermute | solution.py:19
  16.9 133.0 %collective-permute-start.2 = (s32[2]{0:T(128)S(1)}, s32[2]{0:T(128)S(1)}, u32[]{:S(2)}, u32[]{:S(2)}) collective-permute-start(s32[2]{0:T(128)S(1)} %bitcast.295), channel_id=1, source_target_pairs={{0,2},{1,3},{2,4},{3,5},{4,6},{5,7},{6,8},{7,9},{8,10},{9,11},{10,... | collective-permute-start | bytes 32 | tf_op jit(solution)/shard_map/ppermute | solution.py:19
  146.5 37.9 %collective-permute-start.5 = (bf16[2,256,1536]{2,1,0:T(8,128)(2,1)}, bf16[2,256,1536]{2,1,0:T(8,128)(2,1)}, u32[]{:S(2)}, u32[]{:S(2)}) collective-permute-start(bf16[2,256,1536]{2,1,0:T(8,128)(2,1)} %bitcast.29), channel_id=1, source_target_pairs={{0,2},{1,3},{2,4},{3,5},{4,6},{5,7},{6,8},{7,9},{8,10},{9,11},{10,... | collective-permute-start | bytes 4718600 | tf_op jit(solution)/shard_map/ppermute | solution.py:19
  156.4 30.7 %collective-permute-start.3 = (bf16[2,256,1536]{2,1,0:T(8,128)(2,1)}, bf16[2,256,1536]{2,1,0:T(8,128)(2,1)}, u32[]{:S(2)}, u32[]{:S(2)}) collective-permute-start(bf16[2,256,1536]{2,1,0:T(8,128)(2,1)} %bitcast.21), channel_id=1, source_target_pairs={{0,14},{1,15},{2,0},{3,1},{4,2},{5,3},{6,4},{7,5},{8,6},{9,7},{10,... | collective-permute-start | bytes 4718600 | tf_op jit(solution)/shard_map/ppermute | solution.py:19
  159.6 7.5 %copy-start.4 = (pred[64,8,4,128]{3,1,2,0:T(8,128)(4,1)}, pred[64,8,4,128]{3,1,2,0:T(8,128)(4,1)S(1)}, u32[]{:S(2)}) copy-start(pred[64,8,4,128]{3,1,2,0:T(8,128)(4,1)S(1)} %copy.143) | copy-start | bytes 786436
  195.7 1.3 copy-start.9
  197.0 21.0 %copy-start = (f32[12,256,512]{2,1,0:T(8,128)}, f32[12,256,512]{2,1,0:T(8,128)S(1)}, u32[]{:S(2)}) copy-start(f32[12,256,512]{2,1,0:T(8,128)S(1)} %get-tuple-element.42) | copy-start | bytes 18874372
  198.4 18.1 %copy-start.1 = (f32[12,256,512]{2,1,0:T(8,128)}, f32[12,256,512]{2,1,0:T(8,128)S(1)}, u32[]{:S(2)}) copy-start(f32[12,256,512]{2,1,0:T(8,128)S(1)} %get-tuple-element.44) | copy-start | bytes 18874372
  207.1 2.4 copy-start.6
  209.4 7.0 %copy-start.12 = (f32[12,512]{1,0:T(8,128)S(1)}, f32[12,512]{1,0:T(8,128)}, u32[]{:S(2)}) copy-start(f32[12,512]{1,0:T(8,128)} %get-tuple-element.49) | copy-start | bytes 73732
  219.6 10.7 %slice-start = ((s8[12582912]{0:T(1024)(128)(4,1)}), s8[4194304]{0:T(1024)(128)(4,1)S(1)}, s32[]{:S(2)}) async-start(s8[12582912]{0:T(1024)(128)(4,1)} %bitcast.257), calls=%async_computation.1 | async-start | bytes 8388608
  219.6 10.7 %slice-start.1 = ((s8[12582912]{0:T(1024)(128)(4,1)}), s8[4194304]{0:T(1024)(128)(4,1)S(1)}, s32[]{:S(2)}) async-start(s8[12582912]{0:T(1024)(128)(4,1)} %bitcast.257), calls=%async_computation.2 | async-start | bytes 8388608
  227.1 3.2 %slice-start.2 = ((s8[12582912]{0:T(1024)(128)(4,1)}), s8[4194304]{0:T(1024)(128)(4,1)S(1)}, s32[]{:S(2)}) async-start(s8[12582912]{0:T(1024)(128)(4,1)} %bitcast.257), calls=%async_computation.3 | async-start | bytes 8388608
  227.1 3.2 %copy-start.5 = (pred[64,8,4,128]{3,1,2,0:T(8,128)(4,1)S(1)}, pred[64,8,4,128]{3,1,2,0:T(8,128)(4,1)}, u32[]{:S(2)}) copy-start(pred[64,8,4,128]{3,1,2,0:T(8,128)(4,1)} %copy-done.4) | copy-start | bytes 786436
  227.1 6.5 %slice-start.3 = ((s8[6291456]{0:T(1024)(128)(4,1)}), s8[4194304]{0:T(1024)(128)(4,1)S(1)}, s32[]{:S(2)}) async-start(s8[6291456]{0:T(1024)(128)(4,1)} %bitcast.259), calls=%async_computation.4 | async-start | bytes 8388608
  230.4 3.3 %slice-start.4 = ((s8[6291456]{0:T(1024)(128)(4,1)}), s8[2097152]{0:T(1024)(128)(4,1)S(1)}, s32[]{:S(2)}) async-start(s8[6291456]{0:T(1024)(128)(4,1)} %bitcast.259), calls=%async_computation.5 | async-start | bytes 4194304
  230.4 3.3 %copy-start.11 = (bf16[1,256,1536]{1,2,0:T(8,128)(2,1)S(1)}, bf16[1,256,1536]{1,2,0:T(8,128)(2,1)}, u32[]{:S(2)}) copy-start(bf16[1,256,1536]{1,2,0:T(8,128)(2,1)} %copy.103) | copy-start | bytes 2359300
  233.6 3.8 %copy-start.7 = (pred[64,8,4,128]{3,1,2,0:T(8,128)(4,1)S(1)}, pred[64,8,4,128]{3,1,2,0:T(8,128)(4,1)}, u32[]{:S(2)}) copy-start(pred[64,8,4,128]{3,1,2,0:T(8,128)(4,1)} %copy.142) | copy-start | bytes 786436
  233.6 3.7 %copy-start.8 = (bf16[1,512,1536]{1,2,0:T(8,128)(2,1)S(1)}, bf16[1,512,1536]{1,2,0:T(8,128)(2,1)}, u32[]{:S(2)}) copy-start(bf16[1,512,1536]{1,2,0:T(8,128)(2,1)} %get-tuple-element.25) | copy-start | bytes 4718596
  247.2 6.3 %copy-start.3 = (bf16[512,1536]{0,1:T(8,128)(2,1)S(1)}, bf16[512,1536]{0,1:T(8,128)(2,1)}, u32[]{:S(2)}) copy-start(bf16[512,1536]{0,1:T(8,128)(2,1)} %copy-done.2) | copy-start | bytes 4718596
  253.5 4.9 %copy-start.10 = (bf16[1,256,1536]{1,2,0:T(8,128)(2,1)S(1)}, bf16[1,256,1536]{1,2,0:T(8,128)(2,1)}, u32[]{:S(2)}) copy-start(bf16[1,256,1536]{1,2,0:T(8,128)(2,1)} %copy.110) | copy-start | bytes 2359300
  253.5 4.9 %copy-start.14 = (f32[12,128,512]{2,1,0:T(8,128)S(1)}, f32[12,128,512]{2,1,0:T(8,128)}, u32[]{:S(2)}) copy-start(f32[12,128,512]{2,1,0:T(8,128)} %fusion.26) | copy-start | bytes 9437188
  253.5 4.9 %copy-start.15 = (f32[12,128,512]{2,1,0:T(8,128)S(1)}, f32[12,128,512]{2,1,0:T(8,128)}, u32[]{:S(2)}) copy-start(f32[12,128,512]{2,1,0:T(8,128)} %fusion.11) | copy-start | bytes 9437188
Sparse Core Ops, SparseCore 0:
  18.6 115.1 all-gather.1
where the time goes:
time: 287 us; the launch traced here: 283 us
  waiting for transfers between devices  132 us (46%)
  matrix products  61.9 us (22%)
  local copies, waits for them, and re-layouts  39.5 us (14%)
  other arithmetic  28.1 us (10%)
  between operations  13.9 us (5%)
  starting transfers between devices  8.01 us (3%)
    ppermute x6, waiting for transfers between devices, shifted(): return lax.ppermute(value, axis, pairs)  132 us
    dot_general x5, matrix products, absorb(): jnp.einsum('hqk,khe->qhe', rounded_probs, value_heads, preferred_element_...  32.2 us
    dot_general x5, matrix products, absorb(): jnp.einsum('qhe,khe->hqk', query_heads, key_heads, preferred_element_type...  19.4 us
    reduce_sum x5, other arithmetic, absorb(): jnp.sum(weights, axis=(3, 4)).reshape(head_count, tok_rows)  16.9 us
    dot_general x1, matrix products, local(): jnp.dot(attention, lax.all_gather(out_weight, 'blk', axis=1, tiled=True),...  10.2 us
    slice x2, local copies, waits for them, and re-layouts, local(): carried = absorb(carried, queries, arrived[0], arrived[1], columns(offset))  8.67 us
    ppermute x6, starting transfers between devices, shifted(): return lax.ppermute(value, axis, pairs)  8.01 us
    gather x2, local copies, waits for them, and re-layouts, local(): jnp.take(blocked, requests, axis=1)  7.43 us
  transfers between devices with their start and end apart: 7, of which 2 were waited for; matrix products, arithmetic and copies ran while one was open for 40% of the time, Pallas kernels for 0%

commit v1 on v0

v1 whole, which is shorter than its diff:
```python
import functools
import math

import jax
import jax.numpy as jnp
from jax import lax
from jax.experimental import pallas as pl
from jax.experimental.pallas import tpu as pltpu
from jax.sharding import PartitionSpec as P

HEADS = 12
BLOCK = 128
RADIUS = 2
NEG = -1e30
OWN, ACROSS, ALONG, SIBLING, RELAYED = range(5)


def nt_dot(a, b):
    return lax.dot_general(a, b, (((1,), (1,)), ((), ())), preferred_element_type=jnp.float32)


def attend_kernel(
    slabs, q_hbm, k_hbm, v_hbm, bias_ref, out_ref,
    q_buf, kv_buf, score_buf, send_sem, recv_sem, load_sem,
):
    tok, feat = q_hbm.shape
    head = feat // HEADS
    rows = min(256, tok)
    blocks = rows // BLOCK
    factor = math.log2(math.e) / math.sqrt(head)
    s = lax.axis_index("blk")
    c = lax.rem(s, 2)
    y = lax.rem(s // 2, 2)
    sibling = s + 1 - 2 * c
    across = s + 2 - 4 * y
    along_to = lax.rem(s + 4 - 8 * y + slabs, slabs)
    along_from = lax.rem(s - 4 + 8 * y + slabs, slabs)
    late = lax.rem(y + c, 2)

    def cols(h):
        return pl.ds(pl.multiple_of(h * head, head), head)

    def load(h, which):
        src = (k_hbm, v_hbm, q_hbm)[which]
        dst = q_buf.at[h] if which == 2 else kv_buf.at[OWN, which, h]
        return pltpu.make_async_copy(src.at[:, cols(h)], dst, load_sem.at[h, which])

    def send(kind, h, which, source, target):
        return pltpu.make_async_remote_copy(
            src_ref=source,
            dst_ref=kv_buf.at[kind, which, h],
            send_sem=send_sem.at[kind - 1, h, which],
            recv_sem=recv_sem.at[kind - 1, h, which],
            device_id={"blk": target},
            device_id_type=pl.DeviceIdType.MESH,
        )

    def own_send(kind, h, which, target):
        return send(kind, h, which, (k_hbm, v_hbm)[which].at[:, cols(h)], target)

    def pass_on(kind, held, h, which, target):
        return send(kind, h, which, kv_buf.at[held, which, h], target)

    def arrived(kind, h):
        for which in range(2):
            own_send(kind, h, which, sibling).wait_recv()

    barrier = pltpu.get_barrier_semaphore()
    for device in (sibling, across, along_to, along_from):
        pl.semaphore_signal(
            barrier, inc=1, device_id={"blk": device}, device_id_type=pl.DeviceIdType.MESH
        )
    pl.semaphore_wait(barrier, 4)

    def begin(h, carry):
        for which in range(2):
            own_send(ACROSS, h, which, across).start()
        for which in range(2):
            own_send(SIBLING, h, which, sibling).start()
        for which in range(3):
            load(h, which).start()
        return carry

    lax.fori_loop(0, HEADS, begin, 0)

    def head_rows(h, part):
        first = pl.multiple_of(part * rows, rows)
        q = q_buf[h, pl.ds(first, rows), :]
        peak = jnp.full((rows, 128), NEG, jnp.float32)
        for j in range(5):
            raw = nt_dot(q, kv_buf[j, 0, h]) * factor
            for b in range(blocks):
                for n in range(tok // BLOCK):
                    col = j * tok + n * BLOCK
                    piece = raw[b * BLOCK : (b + 1) * BLOCK, n * BLOCK : (n + 1) * BLOCK]
                    piece = piece + bias_ref[part * blocks + b, :, col : col + BLOCK]
                    score_buf[b * BLOCK : (b + 1) * BLOCK, col : col + BLOCK] = piece
            for n in range(tok // BLOCK):
                col = j * tok + n * BLOCK
                peak = jnp.maximum(peak, score_buf[:, col : col + BLOCK])
        top = jnp.max(peak, axis=1, keepdims=True)
        mass = jnp.zeros((rows, 128), jnp.float32)
        total = jnp.zeros((rows, head), jnp.float32)
        for j in range(5):
            weights = jnp.exp2(score_buf[:, j * tok : (j + 1) * tok] - top)
            for n in range(tok // BLOCK):
                mass = mass + weights[:, n * BLOCK : (n + 1) * BLOCK]
            total = total + jnp.dot(
                weights.astype(jnp.bfloat16), kv_buf[j, 1, h], preferred_element_type=jnp.float32
            )
        result = total / jnp.sum(mass, axis=1, keepdims=True)
        out_ref[pl.ds(first, rows), cols(h)] = result.astype(out_ref.dtype)

    def step(i, carry):
        @pl.when(i < HEADS)
        def _():
            arrived(ACROSS, i)
            for which in range(2):
                pass_on(ALONG, ACROSS, i, which, along_to).start()

            @pl.when(late == 0)
            def _():
                for which in range(2):
                    pass_on(RELAYED, ACROSS, i, which, sibling).start()

        @pl.when((i >= 1) & (i < HEADS + 1) & (late == 1))
        def _():
            h = i - 1
            arrived(ALONG, h)
            for which in range(2):
                pass_on(RELAYED, ALONG, h, which, sibling).start()

        @pl.when(i >= 2)
        def _():
            h = i - 2
            for which in range(3):
                load(h, which).wait()
            arrived(SIBLING, h)

            @pl.when(late == 0)
            def _():
                arrived(ALONG, h)

            arrived(RELAYED, h)

            def part_step(part, carry):
                head_rows(h, part)
                return carry

            lax.fori_loop(0, tok // rows, part_step, 0)

        return carry

    lax.fori_loop(0, HEADS + 2, step, 0)

    def finish(h, carry):
        for kind in (ACROSS, ALONG, SIBLING, RELAYED):
            for which in range(2):
                own_send(kind, h, which, sibling).wait_send()
        return carry

    lax.fori_loop(0, HEADS, finish, 0)


def attend(slabs, queries, key_rows, value_rows, bias):
    tok, feat = queries.shape
    head = feat // HEADS
    return pl.pallas_call(
        functools.partial(attend_kernel, slabs),
        out_shape=jax.ShapeDtypeStruct((tok, feat), jnp.bfloat16),
        in_specs=[pl.BlockSpec(memory_space=pl.ANY)] * 3
        + [pl.BlockSpec(memory_space=pltpu.VMEM)],
        out_specs=pl.BlockSpec(memory_space=pltpu.VMEM),
        scratch_shapes=[
            pltpu.VMEM((HEADS, tok, head), jnp.bfloat16),
            pltpu.VMEM((5, 2, HEADS, tok, head), jnp.bfloat16),
            pltpu.VMEM((min(256, tok), 5 * tok), jnp.float32),
            pltpu.SemaphoreType.DMA((4, HEADS, 2)),
            pltpu.SemaphoreType.DMA((4, HEADS, 2)),
            pltpu.SemaphoreType.DMA((HEADS, 3)),
        ],
        compiler_params=pltpu.CompilerParams(
            collective_id=0, has_side_effects=True, vmem_limit_bytes=60 * 2**20
        ),
    )(queries, key_rows, value_rows, bias)


def local(slabs, queries, key_rows, value_rows, block_mask, out_weight):
    s = lax.axis_index("blk")
    c = s % 2
    y = (s // 2) % 2
    per_slab = queries.shape[0] // BLOCK
    table = jnp.where(block_mask > 0, 0.0, NEG).astype(jnp.float32)
    table = table.reshape(block_mask.shape[0], 2 * RADIUS + 1, per_slab)
    back2, back1, own, next1, next2 = (table[:, d] for d in range(5))
    ordered = jnp.concatenate(
        (
            own,
            jnp.where(y == 0, next2, back2),
            jnp.where(y == 0, back2, next2),
            jnp.where(c == 0, next1, back1),
            jnp.where(c == 0, back1, next1),
        ),
        axis=1,
    )
    bias = jnp.repeat(ordered, BLOCK, axis=1)[:, None, :]
    attention = attend(slabs, queries, key_rows, value_rows, bias)
    weight = lax.all_gather(out_weight, "blk", axis=1, tiled=True)
    return jnp.dot(attention, weight, preferred_element_type=jnp.float32).astype(jnp.bfloat16)


def solution(mesh):
    in_specs = (
        P(("groups", "blk"), None),
        P(("groups", "blk"), None),
        P(("groups", "blk"), None),
        P("blk", None),
        P(None, "blk"),
    )
    out_specs = P(("groups", "blk"), None)
    body = functools.partial(local, mesh.shape["blk"])
    return jax.shard_map(body, mesh=mesh, in_specs=in_specs, out_specs=out_specs, check_vma=False)
```

time: 287 us -> 176 us (0.61)
  Pallas kernels: 0 us -> 105 us
  waiting for transfers between devices: 132 us -> 43.5 us
  matrix products: 61.9 us -> 9.26 us
  local copies, waits for them, and re-layouts: 39.5 us -> 0.92 us
  other arithmetic: 28.1 us -> 0.7 us
  starting transfers between devices: 8.01 us -> 0.01 us
    ppermute x6 -> x0, waiting for transfers between devices: 132 us -> none  [shifted(): return lax.ppermute(value, axis, pairs)]
    pallas_call x0 -> x1, Pallas kernels: none -> 105 us  [attend(): pl.pallas_call(functools.partial(attend_kernel, slabs), out_shape=jax.Sha...]
    dot_general x11 -> x1, matrix products: 61.9 us -> 9.26 us  [local(): jnp.dot(attention, weight, preferred_element_type=jnp.float32)]
    all_gather x1, waiting for transfers between devices: 0.02 us -> 42.8 us  [local(): weight = lax.all_gather(out_weight, 'blk', axis=1, tiled=True)]
    slice x8 -> x0, local copies, waits for them, and re-layouts: 19.9 us -> none  [the longest x2 8.67 us: local(): carried = absorb(carried, queries, arrived[0], arrived[1], columns(offset))]
    reduce_sum x5 -> x0, other arithmetic: 16.9 us -> none  [absorb(): jnp.sum(weights, axis=(3, 4)).reshape(head_count, tok_rows)]
    gather x4 -> x0, local copies, waits for them, and re-layouts: 8.55 us -> none  [the longest x2 7.43 us: local(): jnp.take(blocked, requests, axis=1)]
    ppermute x6 -> x0, starting transfers between devices: 8.01 us -> none  [shifted(): return lax.ppermute(value, axis, pairs)]
  transfers between devices with their start and end apart: 7 -> 1, of which waited for: 2 -> 1; matrix products, arithmetic and copies ran while one was open for 40% -> 1% of each run, Pallas kernels for 0% -> 61%
where the time goes in v1:
time: 176 us; the launch traced here: 173 us
  Pallas kernels  105 us (60%)
  waiting for transfers between devices  43.5 us (25%)
  between operations  13.4 us (8%)
  matrix products  9.26 us (5%)
    pallas_call x1, Pallas kernels, attend(): pl.pallas_call(functools.partial(attend_kernel, slabs), out_shape=jax.Sha...  105 us
    all_gather x1, waiting for transfers between devices, local(): weight = lax.all_gather(out_weight, 'blk', axis=1, tiled=True)  42.8 us
    dot_general x1, matrix products, local(): jnp.dot(attention, weight, preferred_element_type=jnp.float32)  9.26 us
  transfers between devices with their start and end apart: 1, of which 1 were waited for; matrix products, arithmetic and copies ran while one was open for 1% of the time, Pallas kernels for 61%

profile of v1, /device:TPU:12, one launch (start us, length us, event | category | flops | bytes accessed | tf_op | source)
XLA Modules:
  0.0 173.2 jit_solution(14289068835911703344)
XLA Ops:
  6.5 0.0 all-gather.2.cloned.1.call-start
  6.5 0.7 all-gather.2.cloned.1.call-update
  7.3 0.7 compare_select_fusion
  8.0 0.1 reshape.11
  8.1 0.1 concatenate.3
  8.2 0.1 broadcast_in_dim.13
  8.2 0.7 broadcast_in_dim_reshape.4.bias_ref
  8.9 105.4 %shard_map.55 = bf16[512,1536]{1,0:T(8,128)(2,1)} custom-call(bf16[512,1536]{1,0:T(8,128)(2,1)} %q_hbm.1, bf16[512,1536]{1,0:T(8,128)(2,1)} %k_hbm.1, bf16[512,1536]{1,0:T(8,128)(2,1)} %v_hbm.1, f32[4,1,2560]{2,1,0:T(1,128)} %broadcast_in_dim_reshape.4.bias_ref), custom_call_target="tpu_custom_call" | custom-call | tf_op jit(solution)/shard_map/pallas_call | solution.py:168
  114.3 42.8 %all-gather.2.cloned.1.call-done = bf16[1536,3072]{0,1:T(8,128)(2,1)} async-done(((bf16[1536,192]{0,1:T(8,128)(2,1)}), bf16[1536,3072]{0,1:T(8,128)(2,1)}) %all-gather.2.cloned.1.call-update) | async-done | bytes 9437200 | tf_op jit(solution)/shard_map/all_gather | solution.py:208
  157.0 9.3 %convolution_convert_fusion = bf16[512,3072]{1,0:T(8,128)(2,1)} fusion(bf16[512,1536]{1,0:T(8,128)(2,1)} %shard_map.55, bf16[1536,3072]{0,1:T(8,128)(2,1)} %all-gather.2.cloned.1.call-done), kind=kOutput, calls=%fused_computation | convolution fusion | flops 4833411072 | bytes 14155776 | tf_op jit(solution)/shard_map/dot_general | solution.py:209
  (1 shorter events, 0.0 us)
Async XLA Ops:
  6.5 150.5 %all-gather.2.cloned.1.call-start = ((), (), s32[]{:S(2)}) async-start(), calls=%async_computation | async-start | bytes 10027008 | tf_op jit(solution)/shard_map/all_gather | solution.py:208
Sparse Core Ops, SparseCore 0:
  9.6 147.3 all-gather.1

commit v2 on v1

--- a/solution.py
+++ b/solution.py
@@ -19,16 +19,26 @@
     return lax.dot_general(a, b, (((1,), (1,)), ((), ())), preferred_element_type=jnp.float32)
 
 
-def attend_kernel(
-    slabs, q_hbm, k_hbm, v_hbm, bias_ref, out_ref,
-    q_buf, kv_buf, score_buf, send_sem, recv_sem, load_sem,
-):
+LOOKAHEAD = 4
+EARLY = 8
+
+
+def attend_kernel(slabs, project, *refs):
+    if project:
+        q_hbm, k_hbm, v_hbm, bias_ref, w_hbm, out_ref = refs[:6]
+        q_buf, kv_buf, score_buf, send_sem, recv_sem, load_sem = refs[6:12]
+        heads_ref, w_buf, sum_buf, w_send, w_recv, w_load = refs[12:]
+    else:
+        q_hbm, k_hbm, v_hbm, bias_ref, heads_ref = refs[:5]
+        q_buf, kv_buf, score_buf, send_sem, recv_sem, load_sem = refs[5:]
     tok, feat = q_hbm.shape
     head = feat // HEADS
     rows = min(256, tok)
     blocks = rows // BLOCK
     factor = math.log2(math.e) / math.sqrt(head)
+    quads = slabs // 4
     s = lax.axis_index("blk")
+    g = lax.axis_index("groups")
     c = lax.rem(s, 2)
     y = lax.rem(s // 2, 2)
     sibling = s + 1 - 2 * c
@@ -65,23 +75,86 @@
         for which in range(2):
             own_send(kind, h, which, sibling).wait_recv()
 
+    if project:
+        width = w_hbm.shape[0]
+        half = width // 2
+        far_sibling = across + 1 - 2 * c
+
+        def slot(base, k):
+            return lax.rem(base - 4 * k + slabs, slabs)
+
+        def w_rows(index, part):
+            if part is None:
+                return pl.ds(pl.multiple_of(index * width, 32), width)
+            return pl.ds(pl.multiple_of(index * width + part * half, 32), half)
+
+        def w_copy(sem, k, index, part, target, own=False):
+            place = w_buf.at[w_rows(index, part)]
+            if not own:
+                source = place
+            elif part is None:
+                source = w_hbm
+            else:
+                source = w_hbm.at[pl.ds(pl.multiple_of(part * half, 32), half)]
+            return pltpu.make_async_remote_copy(
+                src_ref=source,
+                dst_ref=place,
+                send_sem=w_send.at[sem, k],
+                recv_sem=w_recv.at[sem, k],
+                device_id=target,
+                device_id_type=pl.DeviceIdType.MESH,
+            )
+
+        def w_along(k, index, target):
+            return w_copy(0, k, index, g, {"blk": target}, own=True)
+
+        def w_across(k, index, own=False):
+            return w_copy(1, k, index, g, {"blk": across}, own=own)
+
+        def w_twin(near, k, index, part):
+            return w_copy(2 + near, k, index, part, {"groups": 1 - g})
+
+        def w_sibling(near, k, index, own=False):
+            return w_copy(4 + near, k, index, None, {"blk": sibling}, own=own)
+
+        w_keep = pltpu.make_async_copy(w_hbm, w_buf.at[w_rows(s, None)], w_load.at[0])
+
     barrier = pltpu.get_barrier_semaphore()
-    for device in (sibling, across, along_to, along_from):
+    if project:
+        peers = [{"blk": sibling}, {"blk": across}, {"groups": 1 - g}]
+        peers += [{"blk": lax.rem(s + 4 * k, slabs)} for k in range(1, quads)]
+    else:
+        peers = [{"blk": device} for device in (sibling, across, along_to, along_from)]
+    for device in peers:
         pl.semaphore_signal(
-            barrier, inc=1, device_id={"blk": device}, device_id_type=pl.DeviceIdType.MESH
+            barrier, inc=1, device_id=device, device_id_type=pl.DeviceIdType.MESH
         )
-    pl.semaphore_wait(barrier, 4)
-
-    def begin(h, carry):
+    pl.semaphore_wait(barrier, len(peers))
+
+    def begin_across(h, carry):
         for which in range(2):
             own_send(ACROSS, h, which, across).start()
+        return carry
+
+    def begin(h, carry):
         for which in range(2):
             own_send(SIBLING, h, which, sibling).start()
         for which in range(3):
             load(h, which).start()
         return carry
 
-    lax.fori_loop(0, HEADS, begin, 0)
+    if project:
+        lax.fori_loop(0, 2, begin_across, 0)
+        for k in range(1, quads):
+            w_along(k, s, lax.rem(s + 4 * k, slabs)).start()
+        w_across(0, s, own=True).start()
+        lax.fori_loop(2, LOOKAHEAD, begin_across, 0)
+        lax.fori_loop(0, HEADS, begin, 0)
+        w_keep.start()
+        w_sibling(1, 0, s, own=True).start()
+    else:
+        lax.fori_loop(0, LOOKAHEAD, begin_across, 0)
+        lax.fori_loop(0, HEADS, begin, 0)
 
     def head_rows(h, part):
         first = pl.multiple_of(part * rows, rows)
@@ -109,7 +182,36 @@
                 weights.astype(jnp.bfloat16), kv_buf[j, 1, h], preferred_element_type=jnp.float32
             )
         result = total / jnp.sum(mass, axis=1, keepdims=True)
-        out_ref[pl.ds(first, rows), cols(h)] = result.astype(out_ref.dtype)
+        heads_ref[pl.ds(first, rows), cols(h)] = result.astype(jnp.bfloat16)
+
+    def weight_step(i):
+        @pl.when((i >= 1) & (i < quads))
+        def _():
+            index = slot(s, i)
+            w_along(i, index, sibling).wait_recv()
+            w_across(i, index).start()
+            w_twin(1, i, index, g).start()
+
+        @pl.when((i >= 2) & (i < quads + 2))
+        def _():
+            k = i - 2
+            index = slot(across, k)
+            w_across(k, index).wait_recv()
+            w_twin(0, k, index, g).start()
+
+        @pl.when((i >= 4) & (i < quads + 3))
+        def _():
+            k = i - 3
+            index = slot(s, k)
+            w_twin(1, k, index, 1 - g).wait_recv()
+            w_sibling(1, k, index).start()
+
+        @pl.when((i >= 4) & (i < quads + 4))
+        def _():
+            k = i - 4
+            index = slot(across, k)
+            w_twin(0, k, index, 1 - g).wait_recv()
+            w_sibling(0, k, index).start()
 
     def step(i, carry):
         @pl.when(i < HEADS)
@@ -123,6 +225,10 @@
                 for which in range(2):
                     pass_on(RELAYED, ACROSS, i, which, sibling).start()
 
+        @pl.when(i + LOOKAHEAD < HEADS)
+        def _():
+            begin_across(i + LOOKAHEAD, 0)
+
         @pl.when((i >= 1) & (i < HEADS + 1) & (late == 1))
         def _():
             h = i - 1
@@ -130,6 +236,9 @@
             for which in range(2):
                 pass_on(RELAYED, ALONG, h, which, sibling).start()
 
+        if project:
+            weight_step(i)
+
         @pl.when(i >= 2)
         def _():
             h = i - 2
@@ -149,9 +258,35 @@
 
             lax.fori_loop(0, tok // rows, part_step, 0)
 
+        if project:
+
+            @pl.when(i == EARLY + 2)
+            def _():
+                w_keep.wait()
+                for k in range(quads):
+                    w_sibling(1, k, slot(sibling, k)).wait_recv()
+                    w_sibling(0, k, slot(far_sibling, k)).wait_recv()
+                lax.fori_loop(0, w_buf.shape[0] // 512, early_tile, 0)
+
         return carry
 
+    if project:
+        cut = EARLY * head
+
+        def early_tile(t, carry):
+            place = pl.ds(pl.multiple_of(t * 512, 512), 512)
+            sum_buf[:, place] = nt_dot(heads_ref[:, :cut], w_buf[place, :cut])
+            return carry
+
+        def last_tile(t, carry):
+            place = pl.ds(pl.multiple_of(t * 512, 512), 512)
+            rest = nt_dot(heads_ref[:, cut:], w_buf[place, cut:])
+            out_ref[:, place] = (sum_buf[:, place] + rest).astype(out_ref.dtype)
+            return carry
+
     lax.fori_loop(0, HEADS + 2, step, 0)
+    if project:
+        lax.fori_loop(0, w_buf.shape[0] // 512, last_tile, 0)
 
     def finish(h, carry):
         for kind in (ACROSS, ALONG, SIBLING, RELAYED):
@@ -160,32 +295,56 @@
         return carry
 
     lax.fori_loop(0, HEADS, finish, 0)
-
-
-def attend(slabs, queries, key_rows, value_rows, bias):
+    if project:
+        for k in range(quads):
+            if k:
+                w_along(k, s, sibling).wait_send()
+                w_twin(1, k, slot(s, k), g).wait_send()
+            w_across(k, slot(s, k)).wait_send()
+            w_twin(0, k, slot(across, k), g).wait_send()
+            w_sibling(1, k, slot(s, k)).wait_send()
+            w_sibling(0, k, slot(across, k)).wait_send()
+
+
+def attend(slabs, project, queries, key_rows, value_rows, bias, weight):
     tok, feat = queries.shape
     head = feat // HEADS
+    scratch = [
+        pltpu.VMEM((HEADS, tok, head), jnp.bfloat16),
+        pltpu.VMEM((5, 2, HEADS, tok, head), jnp.bfloat16),
+        pltpu.VMEM((min(256, tok), 5 * tok), jnp.float32),
+        pltpu.SemaphoreType.DMA((4, HEADS, 2)),
+        pltpu.SemaphoreType.DMA((4, HEADS, 2)),
+        pltpu.SemaphoreType.DMA((HEADS, 3)),
+    ]
+    in_specs = [pl.BlockSpec(memory_space=pl.ANY)] * 3 + [pl.BlockSpec(memory_space=pltpu.VMEM)]
+    operands = [queries, key_rows, value_rows, bias]
+    width = feat
+    if project:
+        width = slabs * weight.shape[0]
+        in_specs.append(pl.BlockSpec(memory_space=pl.ANY))
+        operands.append(weight)
+        scratch += [
+            pltpu.VMEM((tok, feat), jnp.bfloat16),
+            pltpu.VMEM((width, feat), jnp.bfloat16),
+            pltpu.VMEM((tok, width), jnp.float32),
+            pltpu.SemaphoreType.DMA((6, slabs // 4)),
+            pltpu.SemaphoreType.DMA((6, slabs // 4)),
+            pltpu.SemaphoreType.DMA((1,)),
+        ]
     return pl.pallas_call(
-        functools.partial(attend_kernel, slabs),
-        out_shape=jax.ShapeDtypeStruct((tok, feat), jnp.bfloat16),
-        in_specs=[pl.BlockSpec(memory_space=pl.ANY)] * 3
-        + [pl.BlockSpec(memory_space=pltpu.VMEM)],
+        functools.partial(attend_kernel, slabs, project),
+        out_shape=jax.ShapeDtypeStruct((tok, width), jnp.bfloat16),
+        in_specs=in_specs,
         out_specs=pl.BlockSpec(memory_space=pltpu.VMEM),
-        scratch_shapes=[
-            pltpu.VMEM((HEADS, tok, head), jnp.bfloat16),
-            pltpu.VMEM((5, 2, HEADS, tok, head), jnp.bfloat16),
-            pltpu.VMEM((min(256, tok), 5 * tok), jnp.float32),
-            pltpu.SemaphoreType.DMA((4, HEADS, 2)),
-            pltpu.SemaphoreType.DMA((4, HEADS, 2)),
-            pltpu.SemaphoreType.DMA((HEADS, 3)),
-        ],
+        scratch_shapes=scratch,
         compiler_params=pltpu.CompilerParams(
             collective_id=0, has_side_effects=True, vmem_limit_bytes=60 * 2**20
         ),
-    )(queries, key_rows, value_rows, bias)
-
-
-def local(slabs, queries, key_rows, value_rows, block_mask, out_weight):
+    )(*operands)
+
+
+def local(slabs, groups, queries, key_rows, value_rows, block_mask, out_weight):
     s = lax.axis_index("blk")
     c = s % 2
     y = (s // 2) % 2
@@ -204,7 +363,11 @@
         axis=1,
     )
     bias = jnp.repeat(ordered, BLOCK, axis=1)[:, None, :]
-    attention = attend(slabs, queries, key_rows, value_rows, bias)
+    width = out_weight.shape[1]
+    project = groups == 2 and 3 <= slabs // 4 <= 4 and width % 64 == 0 and slabs * width % 512 == 0
+    if project:
+        return attend(slabs, True, queries, key_rows, value_rows, bias, out_weight.T)
+    attention = attend(slabs, False, queries, key_rows, value_rows, bias, None)
     weight = lax.all_gather(out_weight, "blk", axis=1, tiled=True)
     return jnp.dot(attention, weight, preferred_element_type=jnp.float32).astype(jnp.bfloat16)
 
@@ -218,5 +381,5 @@
         P(None, "blk"),
     )
     out_specs = P(("groups", "blk"), None)
-    body = functools.partial(local, mesh.shape["blk"])
+    body = functools.partial(local, mesh.shape["blk"], mesh.shape["groups"])
     return jax.shard_map(body, mesh=mesh, in_specs=in_specs, out_specs=out_specs, check_vma=False)

time: 176 us -> 139 us (0.79); the launches traced: 173 us -> 139 us
  waiting for transfers between devices: 43.5 us -> 0 us
  Pallas kernels: 105 us -> 134 us
  between operations: 13.4 us -> 0.02 us
  matrix products: 9.26 us -> 0 us
  local copies, waits for them, and re-layouts: 0.92 us -> 4.67 us
    all_gather x1 -> x0, waiting for transfers between devices: 42.8 us -> none  [local(): weight = lax.all_gather(out_weight, 'blk', axis=1, tiled=True)]
    pallas_call x1, Pallas kernels: 105 us -> 134 us  [attend(): pl.pallas_call(functools.partial(attend_kernel, slabs, project), out_shap...]
    dot_general x1 -> x0, matrix products: 9.26 us -> none  [local(): jnp.dot(attention, weight, preferred_element_type=jnp.float32)]
    unnamed x0 -> x1, local copies, waits for them, and re-layouts: none -> 3.76 us
  transfers between devices with their start and end apart: 1 -> 0, of which waited for: 1 -> 0; matrix products, arithmetic and copies ran while one was open for 1% -> 0% of each run, Pallas kernels for 61% -> 0%
where the time goes in v2:
time: 139 us
  Pallas kernels  134 us (96%)
  local copies, waits for them, and re-layouts  4.67 us (3%)
    pallas_call x1, Pallas kernels, attend(): pl.pallas_call(functools.partial(attend_kernel, slabs, project), out_shap...  134 us
    unnamed x1, local copies, waits for them, and re-layouts  3.76 us

profile of v2, /device:TPU:12, one launch (start us, length us, event | category | flops | bytes accessed | tf_op | source)
XLA Modules:
  0.0 138.9 jit_solution(11830973255201076956)
XLA Ops:
  0.0 0.7 compare_select_fusion
  0.7 0.1 reshape.11
  0.8 0.1 concatenate.3
  0.9 0.1 broadcast_in_dim.13
  1.0 0.7 broadcast_in_dim_reshape.4.refs_3_
  1.6 133.5 %shard_map.55 = bf16[512,3072]{1,0:T(8,128)(2,1)} custom-call(bf16[512,1536]{1,0:T(8,128)(2,1)} %refs_0_.1, bf16[512,1536]{1,0:T(8,128)(2,1)} %refs_1_.1, bf16[512,1536]{1,0:T(8,128)(2,1)} %refs_2_.1, f32[4,1,2560]{2,1,0:T(1,128)} %broadcast_in_dim_reshape.4.refs_3_, bf16[192,1536]{1,0:T(8,128)(2,1)} %bitcast.6), custom_call_target="tpu_custom_call" | custom-call | tf_op jit(solution)/shard_map/pallas_call | solution.py:335
  135.1 3.8 %copy.8 = bf16[512,3072]{1,0:T(8,128)(2,1)} copy(bf16[512,3072]{1,0:T(8,128)(2,1)} %shard_map.55) | data formatting | bytes 6291456
  (1 shorter events, 0.0 us)
